TPU v7x, 512 devices: a whole 4x8x8 slice. The times are simulated.
512 devices in a mesh: vol: 8 (over z), row: 8 (over y_lo, core), col: 8 (over x, y_hi).
Axes of the slice: x: 4, y: 8 (y_hi: 2, y_lo: 4; y = y_hi * 4 + y_lo), z: 8, core: 2. Of those that a mesh axis runs over, the one named last changes fastest.
Arguments:
- vol_rhs: bfloat16 [64, 786432], P(None, ('vol', 'row', 'col')), may hold values from -6 to 6
- surf_rhs: bfloat16 [64, 65536], P(None, ('vol', 'row', 'col')), may hold values from -6 to 6
- vol_blocks: bfloat16 [6144, 7, 128, 128], P(('vol', 'row', 'col')), may hold values from -0.1875 to 0.1875
- vol_cols: int32 [6144, 7], P(('vol', 'row', 'col')), may hold values from 0 to 11, as said below
- coupling: bfloat16 [2048, 128, 128], P(('vol', 'row', 'col')), may hold values from -0.5 to 0.5
- trace_map: int32 [2048], P(('vol', 'row', 'col')), may hold values from 0 to 7
- bnd_count: int32 [512], P(('vol', 'row', 'col')), may hold values from 1 to 4
- surf_inverse: bfloat16 [512, 128, 128], P(('vol', 'row', 'col')), may hold values from -0.5 to 0.5
- near_blocks: bfloat16 [512, 8, 4, 128, 128], P(('vol', 'row'), 'col'), may hold values from -0.09375 to 0.09375
- near_cols: int32 [512, 8, 4], P(('vol', 'row'), 'col'), may hold values from 0 to 63
- far_u: bfloat16 [8, 32, 65536], P('col', None, ('vol', 'row')), may hold values from -1 to 1
- far_v: bfloat16 [64, 8, 32, 8192], P(('vol', 'row'), 'col'), may hold values from -0.0625 to 0.0625
Outputs:
- vol_field: float32 [64, 786432], P(None, ('vol', 'row', 'col'))
- surf_field: float32 [64, 65536], P(None, ('vol', 'row', 'col'))
Inputs may be any that keep to these rules, and one draw needn't show every extreme that they name: `vol_cols`: row b names 7 different blocks of its own subdomain, the first being b mod 12.
All inputs are finite; a program needn't handle non-finite values.
Results may differ from a plain program's by a relative error of at most 0.01.
Values may be sent and summed in bfloat16 or wider, within the bound.
A program may use at most 64 MiB of HBM per device.

v0:
```python
import jax
import jax.numpy as jnp
from jax import lax
from jax.sharding import PartitionSpec as P

BS = 128
ITERS = 2


def copy_for_each(array, axis):
    devices = lax.axis_size(axis)
    return lax.all_to_all(
        jnp.broadcast_to(array[None], (devices, *array.shape)), axis, 0, 0, tiled=True
    )


def laid_out(tiles, dim):
    shape = list(tiles.shape[1:])
    shape[dim] *= tiles.shape[0]
    return jnp.moveaxis(tiles, 0, dim).reshape(shape)


def gather_directly(array, axis, dim):
    tiles = copy_for_each(array, axis)
    return laid_out(tiles, dim)


def cut_along(array, dim, devices):
    before, after = (array.shape[:dim], array.shape[dim + 1 :])
    return jnp.moveaxis(array.reshape(*before, devices, -1, *after), dim, 0)


def summed_on_arrival(array, axis, dim):
    tiles = cut_along(array, dim, lax.axis_size(axis))
    arrived = lax.all_to_all(tiles, axis, split_axis=0, concat_axis=0, tiled=True)
    return arrived.sum(axis=0)


def volume_solve(field, blocks, columns):
    picked = jnp.take(field, columns, axis=1)
    return jnp.einsum("abnk,bnik->abi", picked, blocks, preferred_element_type=jnp.float32)


def surface_solve(field, blocks):
    return jnp.einsum("abk,bik->abi", field, blocks, preferred_element_type=jnp.float32)


def local(
    vol_rhs,
    surf_rhs,
    vol_blocks,
    vol_cols,
    coupling,
    trace_map,
    bnd_count,
    surf_inverse,
    near_blocks,
    near_cols,
    far_u,
    far_v,
):
    angles = vol_rhs.shape[0]
    vol_count = vol_blocks.shape[0]
    surf_count = surf_inverse.shape[0]
    slot_total = coupling.shape[0]
    piece_rows = surf_count * BS
    vol_size = lax.axis_size("vol")
    row_here = lax.axis_index("row")
    rhs_vol = vol_rhs.astype(jnp.float32).reshape(angles, vol_count, BS)
    rhs_surf = surf_rhs.astype(jnp.float32).reshape(angles, surf_count, BS)
    slot_alive = (jnp.arange(slot_total, dtype=jnp.int32) < bnd_count[0]).astype(jnp.float32)
    selector = (
        trace_map[:, None] == jnp.arange(vol_size * surf_count, dtype=jnp.int32)[None, :]
    ).astype(jnp.float32)
    near_local = near_blocks[:, 0]
    near_index = near_cols[:, 0]
    u_local = far_u[0]
    v_local = far_v[0, 0]
    padding = jnp.zeros((angles, vol_count - slot_total, BS), jnp.float32)
    volume = volume_solve(vol_rhs.reshape(angles, vol_count, BS), vol_blocks, vol_cols)
    surface = surface_solve(surf_rhs.reshape(angles, surf_count, BS), surf_inverse)
    for iteration in range(ITERS):
        x_half = volume.astype(jnp.bfloat16)
        s_half = surface.astype(jnp.bfloat16).reshape(angles, piece_rows)
        column_group = gather_directly(s_half, ("vol", "row"), 1)
        split_group = column_group.reshape(angles, vol_size, -1, piece_rows)
        group_surface = lax.dynamic_index_in_dim(split_group, row_here, 2, keepdims=False).reshape(
            angles, vol_size * piece_rows
        )
        picked = jnp.take(
            group_surface.reshape(angles, vol_size * surf_count, BS), trace_map, axis=1
        )
        current = (
            jnp.einsum("ajk,jik->aji", picked, coupling, preferred_element_type=jnp.float32)
            * slot_alive[None, :, None]
        )
        resid_vol = (rhs_vol - jnp.concatenate([current, padding], axis=1)).astype(jnp.bfloat16)
        contrib = (
            jnp.einsum(
                "aji,jik->jak", x_half[:, :slot_total], coupling, preferred_element_type=jnp.float32
            )
            * slot_alive[:, None, None]
        )
        traced = jnp.transpose(
            summed_on_arrival(jnp.einsum("jm,jak->mak", selector, contrib), "vol", 0), (1, 0, 2)
        )
        column_blocks = column_group.reshape(angles, -1, BS)
        gathered = jnp.take(column_blocks, near_index, axis=1)
        near_term = jnp.einsum(
            "abnk,bnik->abi", gathered, near_local, preferred_element_type=jnp.float32
        )
        coeffs = jnp.einsum(
            "ak,qk->aq", column_group, v_local, preferred_element_type=jnp.float32
        ).astype(jnp.bfloat16)
        far_term = jnp.dot(coeffs, u_local, preferred_element_type=jnp.float32)
        row_partial = near_term.reshape(angles, -1) + far_term
        integral = summed_on_arrival(row_partial, "col", 1)
        resid_surf = (rhs_surf - integral.reshape(angles, surf_count, BS) - traced).astype(
            jnp.bfloat16
        )
        volume = volume_solve(resid_vol, vol_blocks, vol_cols)
        surface = surface + surface_solve(resid_surf, surf_inverse)
    return (volume.reshape(angles, vol_count * BS), surface.reshape(angles, piece_rows))


def solution(mesh):
    in_specs = (
        P(None, ("vol", "row", "col")),
        P(None, ("vol", "row", "col")),
        P(("vol", "row", "col"), None, None, None),
        P(("vol", "row", "col"), None),
        P(("vol", "row", "col"), None, None),
        P(("vol", "row", "col")),
        P(("vol", "row", "col")),
        P(("vol", "row", "col"), None, None),
        P(("vol", "row"), "col", None, None, None),
        P(("vol", "row"), "col", None),
        P("col", None, ("vol", "row")),
        P(("vol", "row"), "col", None, None),
    )
    out_specs = (P(None, ("vol", "row", "col")), P(None, ("vol", "row", "col")))
    return jax.shard_map(local, mesh=mesh, in_specs=in_specs, out_specs=out_specs, check_vma=False)
```

profile of v0, /device:TPU:8, one launch (start us, length us, event | category | flops | bytes accessed | tf_op | source)
XLA Modules:
  0.0 164.0 jit_solution(3306626259298423557)
XLA Ops:
  3.6 14.5 %all-to-all-start = ((bf16[64,64,128]{2,1,0:T(8,128)(2,1)}), bf16[64,64,128]{2,1,0:T(8,128)(2,1)}, u32[]{:S(2)}, u32[]{:S(2)}) async-start(bf16[64,64,128]{2,1,0:T(8,128)(2,1)} %broadcast_in_dim.49), calls=%async_computation | async-start | bytes 2097152 | tf_op jit(solution)/shard_map/all_to_all | solution.py:12
  19.5 1.9 %gather_fusion.1 = bf16[84,64,128]{2,1,0:T(8,128)(2,1)} fusion(bf16[64,12,128]{2,0,1:T(8,128)(2,1)S(1)} %copy_bitcast_fusion.1, s32[1024]{0:T(1024)S(1)} %pad_clamp_fusion.1), kind=kCustom, calls=%fused_computation.1.clone | custom fusion | bytes 2752848 | tf_op jit(solution)/shard_map/jit(_take)/gather | solution.py:40
  21.4 1.6 %fusion.46 = bf16[4,64,128]{2,1,0:T(8,128)(2,1)S(1)} fusion(bf16[4,128,128]{2,1,0:T(8,128)(2,1)S(1)} %copy-done.2, bf16[12,7,128,128]{3,2,1,0:T(8,128)(2,1)S(1)} %copy-done, bf16[12,7,64,128]{3,2,1,0:T(8,128)(2,1)} %bitcast.244, pred[12,7]{1,0:T(8,128)(4,1)S(1)} %copy.67, f32[4]{0:T(128)S(1)} %compare_convert_fusion), kind=kOutput, calls=%fused_computation.41 | convolution fusion | flops 185401344 | bytes 4325476 | tf_op jit(solution)/shard_map/aji,jik->jak/dot_general | solution.py:99
  24.2 22.9 %all-to-all-done = bf16[64,64,128]{2,1,0:T(8,128)(2,1)} async-done(((bf16[64,64,128]{2,1,0:T(8,128)(2,1)}), bf16[64,64,128]{2,1,0:T(8,128)(2,1)}, u32[]{:S(2)}, u32[]{:S(2)}) %all-to-all-start) | async-done | bytes 1048608 | tf_op jit(solution)/shard_map/all_to_all | solution.py:12
  47.0 4.0 %all-to-all-start.2 = ((f32[8,1,64,128]{3,2,1,0:T(8,128)}), f32[8,1,64,128]{3,2,1,0:T(8,128)}, u32[]{:S(2)}, u32[]{:S(2)}) async-start(f32[8,1,64,128]{3,2,1,0:T(8,128)} %copy.78), calls=%async_computation.2 | async-start | bytes 524288 | tf_op jit(solution)/shard_map/all_to_all | solution.py:35
  51.1 1.9 %gather_fusion = bf16[32,64,128]{2,1,0:T(8,128)(2,1)S(1)} fusion(bf16[64,64,128]{2,0,1:T(8,128)(2,1)} %bitcast.5, s32[1024]{0:T(1024)S(1)} %pad_clamp_fusion.2), kind=kCustom, calls=%fused_computation.clone | custom fusion | bytes 1048704 | tf_op jit(solution)/shard_map/jit(_take)/gather | solution.py:108
  53.0 1.7 %convolution_bitcast_fusion.3 = f32[8,8,8,128]{3,2,1,0:T(8,128)S(1)} fusion(bf16[8,1,4,128,128]{4,3,2,1,0:T(8,128)(2,1)} %param.26, bf16[8,4,64,128]{3,2,1,0:T(8,128)(2,1)S(1)} %bitcast.243, pred[8,4]{1,0:T(8,128)(4,1)S(1)} %copy.69), kind=kOutput, calls=%fused_computation.31 | convolution fusion | flops 67371008 | bytes 1835040 | tf_op jit(solution)/shard_map/abnk,bnik->abi/dot_general | solution.py:109
  54.8 2.1 %fusion.28 = f32[8,8,8,128]{3,2,1,0:T(8,128)S(1)} fusion(bf16[1,1,32,8192]{3,2,1,0:T(8,128)(2,1)} %param.29, f32[8,8,8,128]{3,2,1,0:T(8,128)S(1)} %convolution_bitcast_fusion.3, bf16[1,32,1024]{2,1,0:T(8,128)(2,1)} %param.28, bf16[64,64,128]{2,1,0:T(8,128)(2,1)} %all-to-all-done), kind=kOutput, calls=%fused_computation.29 | convolution fusion | flops 37816320 | bytes 2162688 | tf_op jit(solution)/shard_map/dot_general | solution.py:115
  57.6 6.2 %all-to-all-done.2 = f32[8,1,64,128]{3,2,1,0:T(8,128)} async-done(((f32[8,1,64,128]{3,2,1,0:T(8,128)}), f32[8,1,64,128]{3,2,1,0:T(8,128)}, u32[]{:S(2)}, u32[]{:S(2)}) %all-to-all-start.2) | async-done | bytes 262176 | tf_op jit(solution)/shard_map/all_to_all | solution.py:35
  63.7 6.9 %all-to-all-start.1 = ((f32[8,64,128]{2,1,0:T(8,128)}), f32[8,64,128]{2,1,0:T(8,128)S(1)}, u32[]{:S(2)}, u32[]{:S(2)}) async-start(f32[8,64,128]{2,1,0:T(8,128)} %bitcast.240), calls=%async_computation.1 | async-start | bytes 524288 | tf_op jit(solution)/shard_map/all_to_all | solution.py:35
  71.5 11.8 %all-to-all-done.1 = f32[8,64,128]{2,1,0:T(8,128)S(1)} async-done(((f32[8,64,128]{2,1,0:T(8,128)}), f32[8,64,128]{2,1,0:T(8,128)S(1)}, u32[]{:S(2)}, u32[]{:S(2)}) %all-to-all-start.1) | async-done | bytes 262176 | tf_op jit(solution)/shard_map/all_to_all | solution.py:35
  85.5 5.2 %all-to-all-start.3 = ((bf16[64,64,128]{2,1,0:T(8,128)(2,1)}), bf16[64,64,128]{2,1,0:T(8,128)(2,1)}, u32[]{:S(2)}, u32[]{:S(2)}) async-start(bf16[64,64,128]{2,1,0:T(8,128)(2,1)} %broadcast_in_dim.51), calls=%async_computation.3 | async-start | bytes 2097152 | tf_op jit(solution)/shard_map/all_to_all | solution.py:12
  93.1 25.9 %all-to-all-done.3 = bf16[64,64,128]{2,1,0:T(8,128)(2,1)} async-done(((bf16[64,64,128]{2,1,0:T(8,128)(2,1)}), bf16[64,64,128]{2,1,0:T(8,128)(2,1)}, u32[]{:S(2)}, u32[]{:S(2)}) %all-to-all-start.3) | async-done | bytes 1048608 | tf_op jit(solution)/shard_map/all_to_all | solution.py:12
  121.4 1.9 %gather_fusion.4 = bf16[32,64,128]{2,1,0:T(8,128)(2,1)S(1)} fusion(bf16[64,64,128]{2,0,1:T(8,128)(2,1)} %bitcast.27, s32[1024]{0:T(1024)S(1)} %pad_clamp_fusion.2), kind=kCustom, calls=%fused_computation.3.clone | custom fusion | bytes 1048704 | tf_op jit(solution)/shard_map/jit(_take)/gather | solution.py:108
  123.3 1.7 %convolution_bitcast_fusion.2 = f32[8,8,8,128]{3,2,1,0:T(8,128)S(1)} fusion(bf16[8,1,4,128,128]{4,3,2,1,0:T(8,128)(2,1)} %param.26, bf16[8,4,64,128]{3,2,1,0:T(8,128)(2,1)S(1)} %bitcast.242, pred[8,4]{1,0:T(8,128)(4,1)S(1)} %copy.69), kind=kOutput, calls=%fused_computation.30 | convolution fusion | flops 67371008 | bytes 1835040 | tf_op jit(solution)/shard_map/abnk,bnik->abi/dot_general | solution.py:109
  125.1 2.1 %fusion.27 = f32[8,8,8,128]{3,2,1,0:T(8,128)S(1)} fusion(bf16[1,1,32,8192]{3,2,1,0:T(8,128)(2,1)} %param.29, f32[8,8,8,128]{3,2,1,0:T(8,128)S(1)} %convolution_bitcast_fusion.2, bf16[1,32,1024]{2,1,0:T(8,128)(2,1)} %param.28, bf16[64,64,128]{2,1,0:T(8,128)(2,1)} %all-to-all-done.3), kind=kOutput, calls=%fused_computation.27 | convolution fusion | flops 37816320 | bytes 2162688 | tf_op jit(solution)/shard_map/dot_general | solution.py:115
  127.9 3.4 %all-to-all-start.4 = ((f32[8,64,128]{2,1,0:T(8,128)}), f32[8,64,128]{2,1,0:T(8,128)S(1)}, u32[]{:S(2)}, u32[]{:S(2)}) async-start(f32[8,64,128]{2,1,0:T(8,128)} %bitcast.247), calls=%async_computation.4 | async-start | bytes 524288 | tf_op jit(solution)/shard_map/all_to_all | solution.py:35
  132.5 1.9 %gather_fusion.6 = bf16[84,64,128]{2,1,0:T(8,128)(2,1)} fusion(bf16[64,12,128]{2,0,1:T(8,128)(2,1)S(1)} %get-tuple-element.4, s32[1024]{0:T(1024)S(1)} %pad_clamp_fusion.1), kind=kCustom, calls=%fused_computation.5.clone | custom fusion | bytes 2752848 | tf_op jit(solution)/shard_map/jit(_take)/gather | solution.py:40
  134.4 1.6 fusion.43
  137.1 8.9 %all-to-all-done.4 = f32[8,64,128]{2,1,0:T(8,128)S(1)} async-done(((f32[8,64,128]{2,1,0:T(8,128)}), f32[8,64,128]{2,1,0:T(8,128)S(1)}, u32[]{:S(2)}, u32[]{:S(2)}) %all-to-all-start.4) | async-done | bytes 262176 | tf_op jit(solution)/shard_map/all_to_all | solution.py:35
  146.0 4.1 %all-to-all-start.5 = ((f32[8,1,64,128]{3,2,1,0:T(8,128)}), f32[8,1,64,128]{3,2,1,0:T(8,128)}, u32[]{:S(2)}, u32[]{:S(2)}) async-start(f32[8,1,64,128]{3,2,1,0:T(8,128)} %copy.93), calls=%async_computation.5 | async-start | bytes 524288 | tf_op jit(solution)/shard_map/all_to_all | solution.py:35
  150.0 1.9 %gather_fusion.3 = bf16[84,64,128]{2,1,0:T(8,128)(2,1)} fusion(bf16[64,12,128]{2,0,1:T(8,128)(2,1)S(1)} %get-tuple-element.6, s32[1024]{0:T(1024)S(1)} %pad_clamp_fusion.1), kind=kCustom, calls=%fused_computation.4.clone | custom fusion | bytes 2752848 | tf_op jit(solution)/shard_map/jit(_take)/gather | solution.py:40
  151.9 2.6 %fusion.15 = f32[12,8,8,128]{3,2,1,0:T(8,128)S(1)} fusion(bf16[12,7,128,128]{3,2,1,0:T(8,128)(2,1)S(1)} %copy-done, bf16[12,7,64,128]{3,2,1,0:T(8,128)(2,1)} %bitcast.245, pred[12,7]{1,0:T(8,128)(4,1)S(1)} %copy-done.20), kind=kOutput, calls=%fused_computation.20 | convolution fusion | flops 176848896 | bytes 4522068 | tf_op jit(solution)/shard_map/abnk,bnik->abi/dot_general | solution.py:41
  155.3 7.0 %all-to-all-done.5 = f32[8,1,64,128]{3,2,1,0:T(8,128)} async-done(((f32[8,1,64,128]{3,2,1,0:T(8,128)}), f32[8,1,64,128]{3,2,1,0:T(8,128)}, u32[]{:S(2)}, u32[]{:S(2)}) %all-to-all-start.5) | async-done | bytes 262176 | tf_op jit(solution)/shard_map/all_to_all | solution.py:35
  (84 shorter events, 18.7 us)
Async XLA Ops:
  0.6 20.8 %copy-start = (bf16[12,7,128,128]{3,2,1,0:T(8,128)(2,1)S(1)}, bf16[12,7,128,128]{3,2,1,0:T(8,128)(2,1)}, u32[]{:S(2)}) copy-start(bf16[12,7,128,128]{3,2,1,0:T(8,128)(2,1)} %param.20) | copy-start | bytes 8257540
  2.3 16.5 %copy-start.14 = (s32[8,1,4]{0,2,1:T(4,128)S(1)}, s32[8,1,4]{0,2,1:T(4,128)}, u32[]{:S(2)}) copy-start(s32[8,1,4]{0,2,1:T(4,128)} %param.27) | copy-start | bytes 388
  2.3 16.6 %copy-start.13 = (s32[12,7]{0,1:T(8,128)S(1)}, s32[12,7]{0,1:T(8,128)}, u32[]{:S(2)}) copy-start(s32[12,7]{0,1:T(8,128)} %param.21) | copy-start | bytes 1012
  2.3 17.1 %copy-start.1 = (bf16[64,1536]{1,0:T(8,128)(2,1)S(1)}, bf16[64,1536]{1,0:T(8,128)(2,1)}, u32[]{:S(2)}) copy-start(bf16[64,1536]{1,0:T(8,128)(2,1)} %param.18) | copy-start | bytes 589828
  3.6 43.4 %all-to-all-start = ((bf16[64,64,128]{2,1,0:T(8,128)(2,1)}), bf16[64,64,128]{2,1,0:T(8,128)(2,1)}, u32[]{:S(2)}, u32[]{:S(2)}) async-start(bf16[64,64,128]{2,1,0:T(8,128)(2,1)} %broadcast_in_dim.49), calls=%async_computation | async-start | bytes 2097152 | tf_op jit(solution)/shard_map/all_to_all | solution.py:12
  19.0 2.3 %copy-start.19 = (pred[12,7]{1,0:T(8,128)(4,1)}, pred[12,7]{1,0:T(8,128)(4,1)S(1)}, u32[]{:S(2)}) copy-start(pred[12,7]{1,0:T(8,128)(4,1)S(1)} %copy.67) | copy-start | bytes 256
  19.5 1.9 %copy-start.2 = (bf16[4,128,128]{2,1,0:T(8,128)(2,1)S(1)}, bf16[4,128,128]{2,1,0:T(8,128)(2,1)}, u32[]{:S(2)}) copy-start(bf16[4,128,128]{2,1,0:T(8,128)(2,1)} %param.22) | copy-start | bytes 393220
  21.4 1.7 %copy-start.16 = (f32[4]{0:T(128)}, f32[4]{0:T(128)S(1)}, u32[]{:S(2)}) copy-start(f32[4]{0:T(128)S(1)} %compare_convert_fusion) | copy-start | bytes 52
  47.0 16.7 %all-to-all-start.2 = ((f32[8,1,64,128]{3,2,1,0:T(8,128)}), f32[8,1,64,128]{3,2,1,0:T(8,128)}, u32[]{:S(2)}, u32[]{:S(2)}) async-start(f32[8,1,64,128]{3,2,1,0:T(8,128)} %copy.78), calls=%async_computation.2 | async-start | bytes 524288 | tf_op jit(solution)/shard_map/all_to_all | solution.py:35
  54.7 28.7 %copy-start.6 = (f32[128,64]{0,1:T(8,128)S(1)}, f32[128,64]{0,1:T(8,128)}, u32[]{:S(2)}) copy-start(f32[128,64]{0,1:T(8,128)} %copy-done.5) | copy-start | bytes 98308
  54.7 28.7 %copy-start.7 = (bf16[1,128,128]{2,1,0:T(8,128)(2,1)S(1)}, bf16[1,128,128]{2,1,0:T(8,128)(2,1)}, u32[]{:S(2)}) copy-start(bf16[1,128,128]{2,1,0:T(8,128)(2,1)} %param.25) | copy-start | bytes 98308
  54.7 28.7 %copy-start.11 = (bf16[64,128]{1,0:T(8,128)(2,1)S(1)}, bf16[64,128]{1,0:T(8,128)(2,1)}, u32[]{:S(2)}) copy-start(bf16[64,128]{1,0:T(8,128)(2,1)} %param.19) | copy-start | bytes 49156
  63.7 19.7 %all-to-all-start.1 = ((f32[8,64,128]{2,1,0:T(8,128)}), f32[8,64,128]{2,1,0:T(8,128)S(1)}, u32[]{:S(2)}, u32[]{:S(2)}) async-start(f32[8,64,128]{2,1,0:T(8,128)} %bitcast.240), calls=%async_computation.1 | async-start | bytes 524288 | tf_op jit(solution)/shard_map/all_to_all | solution.py:35
  85.5 6.8 %copy-start.3 = (bf16[4,128,128]{2,1,0:T(8,128)(2,1)S(1)}, bf16[4,128,128]{2,1,0:T(8,128)(2,1)}, u32[]{:S(2)}) copy-start(bf16[4,128,128]{2,1,0:T(8,128)(2,1)} %param.22) | copy-start | bytes 393220
  85.5 6.8 %copy-start.17 = (f32[4]{0:T(128)S(1)}, f32[4]{0:T(128)}, u32[]{:S(2)}) copy-start(f32[4]{0:T(128)} %copy-done.16) | copy-start | bytes 52
  85.5 33.6 %all-to-all-start.3 = ((bf16[64,64,128]{2,1,0:T(8,128)(2,1)}), bf16[64,64,128]{2,1,0:T(8,128)(2,1)}, u32[]{:S(2)}, u32[]{:S(2)}) async-start(bf16[64,64,128]{2,1,0:T(8,128)(2,1)} %broadcast_in_dim.51), calls=%async_computation.3 | async-start | bytes 2097152 | tf_op jit(solution)/shard_map/all_to_all | solution.py:12
  127.9 18.1 %all-to-all-start.4 = ((f32[8,64,128]{2,1,0:T(8,128)}), f32[8,64,128]{2,1,0:T(8,128)S(1)}, u32[]{:S(2)}, u32[]{:S(2)}) async-start(f32[8,64,128]{2,1,0:T(8,128)} %bitcast.247), calls=%async_computation.4 | async-start | bytes 524288 | tf_op jit(solution)/shard_map/all_to_all | solution.py:35
  132.4 1.9 %copy-start.4 = (bf16[4,128,128]{2,1,0:T(8,128)(2,1)S(1)}, bf16[4,128,128]{2,1,0:T(8,128)(2,1)}, u32[]{:S(2)}) copy-start(bf16[4,128,128]{2,1,0:T(8,128)(2,1)} %param.22) | copy-start | bytes 393220
  132.4 1.9 %copy-start.18 = (f32[4]{0:T(128)S(1)}, f32[4]{0:T(128)}, u32[]{:S(2)}) copy-start(f32[4]{0:T(128)} %copy-done.16) | copy-start | bytes 52
  132.4 1.9 %copy-start.20 = (pred[12,7]{1,0:T(8,128)(4,1)S(1)}, pred[12,7]{1,0:T(8,128)(4,1)}, u32[]{:S(2)}) copy-start(pred[12,7]{1,0:T(8,128)(4,1)} %copy-done.19) | copy-start | bytes 256
  146.0 16.3 %all-to-all-start.5 = ((f32[8,1,64,128]{3,2,1,0:T(8,128)}), f32[8,1,64,128]{3,2,1,0:T(8,128)}, u32[]{:S(2)}, u32[]{:S(2)}) async-start(f32[8,1,64,128]{3,2,1,0:T(8,128)} %copy.93), calls=%async_computation.5 | async-start | bytes 524288 | tf_op jit(solution)/shard_map/all_to_all | solution.py:35
  154.5 8.8 %copy-start.8 = (bf16[1,128,128]{2,1,0:T(8,128)(2,1)S(1)}, bf16[1,128,128]{2,1,0:T(8,128)(2,1)}, u32[]{:S(2)}) copy-start(bf16[1,128,128]{2,1,0:T(8,128)(2,1)} %param.25) | copy-start | bytes 98308
  154.5 8.8 %copy-start.10 = (f32[128,64]{0,1:T(8,128)S(1)}, f32[128,64]{0,1:T(8,128)}, u32[]{:S(2)}) copy-start(f32[128,64]{0,1:T(8,128)} %copy-done.9) | copy-start | bytes 98308
  154.5 8.8 %copy-start.12 = (bf16[64,128]{1,0:T(8,128)(2,1)S(1)}, bf16[64,128]{1,0:T(8,128)(2,1)}, u32[]{:S(2)}) copy-start(bf16[64,128]{1,0:T(8,128)(2,1)} %param.19) | copy-start | bytes 49156
  (3 other events, 3.0 us)
where the time goes:
time: 165 us; the launch traced here: 164 us
  waiting for transfers between devices  82.6 us (50%)
  starting transfers between devices  38.1 us (23%)
  local copies, waits for them, and re-layouts  20.6 us (12%)
  matrix products  17.8 us (11%)
  other arithmetic  3.18 us (2%)
  between operations  1.73 us (1%)
    all_to_all x2, waiting for transfers between devices, copy_for_each(): lax.all_to_all(jnp.broadcast_to(array[None], (devices, *array.shape)), ax...  48.8 us
    all_to_all x4, waiting for transfers between devices, summed_on_arrival(): lax.all_to_all(tiles, axis, split_axis=0, concat_axis=0, tiled=True)  33.8 us
    all_to_all x2, starting transfers between devices, copy_for_each(): lax.all_to_all(jnp.broadcast_to(array[None], (devices, *array.shape)), ax...  19.8 us
    all_to_all x4, starting transfers between devices, summed_on_arrival(): lax.all_to_all(tiles, axis, split_axis=0, concat_axis=0, tiled=True)  18.4 us
    gather x3, local copies, waits for them, and re-layouts, volume_solve(): picked = jnp.take(field, columns, axis=1)  5.66 us
    dot_general x2, matrix products, local(): far_term = jnp.dot(coeffs, u_local, preferred_element_type=jnp.float32)  4.13 us
    gather x2, local copies, waits for them, and re-layouts, local(): gathered = jnp.take(column_blocks, near_index, axis=1)  3.74 us
    dot_general x2, matrix products, local(): jnp.einsum('abnk,bnik->abi', gathered, near_local, preferred_element_type...  3.48 us
  transfers between devices with their start and end apart: 6, of which 6 were waited for; matrix products, arithmetic and copies ran while one was open for 16% of the time, Pallas kernels for 0%

commit v1 on v0

v1 whole, which is shorter than its diff:
```python
import functools

import jax
import jax.numpy as jnp
from jax import lax
from jax.experimental import pallas as pl
from jax.experimental.pallas import tpu as pltpu
from jax.sharding import PartitionSpec as P

BS = 128
ITERS = 2
CORES = 2
Y_HALVES = 2
MESH = pl.DeviceIdType.MESH
F32 = jnp.float32
BF16 = jnp.bfloat16


def dot_nt(a, b):
    return lax.dot_general(a, b, (((1,), (1,)), ((), ())), preferred_element_type=F32)


def dot_nn(a, b):
    return lax.dot_general(a, b, (((1,), (0,)), ((), ())), preferred_element_type=F32)


def kernel(
    sizes,
    vol_cols,
    trace_map,
    bnd_count,
    near_cols,
    vol_rhs,
    surf_rhs,
    vol_blocks,
    coupling,
    surf_inverse,
    near_blocks,
    far_u,
    far_v,
    vol_out,
    surf_out,
    rhs4,
    field,
    rhs_surf,
    blocks,
    couple,
    inverse,
    near,
    u_mat,
    v_mat,
    gat_a0,
    gat_b0,
    gat_a1,
    gat_b1,
    tr_send,
    tr_recv,
    row_send,
    row_recv,
    row_own,
    surface,
    vol_res,
    load_sem,
    store_sem,
    a1_send,
    a1_recv,
    b1_send,
    b1_recv,
    a2_send,
    a2_recv,
    b2_send,
    b2_recv,
    ca_send,
    ca_recv,
    cb_send,
    cb_recv,
    tr_ssem,
    tr_rsem,
    row_ssem,
    row_rsem,
):
    gat_a, gat_b = (gat_a0, gat_a1), (gat_b0, gat_b1)
    nz, ny, nx = sizes
    ncol = nx * Y_HALVES
    angles = rhs_surf.shape[0]
    half = angles // 2
    nblk = field.shape[0]
    nnz = blocks.shape[1]
    slots = couple.shape[0]
    nears = near.shape[1]

    z = lax.axis_index("vol")
    row = lax.axis_index("row")
    col = lax.axis_index("col")
    y, core = row // CORES, row % CORES
    x, y_hi = col // Y_HALVES, col % Y_HALVES

    def z_peer(o):
        return lax.rem(z + o, nz)

    def y_peer(o):
        return lax.rem(y + o, ny)

    def col_peer(o):
        return lax.rem(x + o // Y_HALVES, nx) * Y_HALVES + lax.rem(y_hi + o % Y_HALVES, Y_HALVES)

    partner = y * CORES + (1 - core)

    loads = []

    def load(src, dst):
        copy = pltpu.make_async_copy(src, dst, load_sem.at[len(loads)])
        copy.start()
        loads.append(copy)
        return copy

    ld_rhs_surf = load(surf_rhs, rhs_surf)
    ld_inverse = load(surf_inverse.at[0], inverse)

    barrier = pltpu.get_barrier_semaphore()
    for o in range(1, nz):
        pl.semaphore_signal(barrier, inc=1, device_id={"vol": z_peer(o)}, device_id_type=MESH)
    for o in range(1, ny):
        pl.semaphore_signal(
            barrier, inc=1, device_id={"row": y_peer(o) * CORES + core}, device_id_type=MESH
        )
    pl.semaphore_signal(barrier, inc=1, device_id={"row": partner}, device_id_type=MESH)
    for o in range(1, ncol):
        pl.semaphore_signal(barrier, inc=1, device_id={"col": col_peer(o)}, device_id_type=MESH)

    ld_field = [load(vol_rhs.at[:, b * BS : (b + 1) * BS], field.at[b]) for b in range(nblk)]
    ld_rhs4 = [load(vol_rhs.at[:, b * BS : (b + 1) * BS], rhs4.at[b]) for b in range(slots)]
    ld_blocks = load(vol_blocks.at[0:slots], blocks.at[0:slots])
    ld_couple = load(coupling, couple)
    ld_v = load(far_v.at[0, 0], v_mat)
    ld_u = load(far_u.at[0], u_mat)
    ld_near = load(near_blocks.at[:, 0], near)
    ld_rest = load(vol_blocks.at[slots:nblk], blocks.at[slots:nblk])

    ld_rhs_surf.wait()
    ld_inverse.wait()
    surface[...] = dot_nt(rhs_surf[...], inverse[...])

    sends = []

    def send(src, dst, ssem, rsem, device):
        copy = pltpu.make_async_remote_copy(
            src_ref=src, dst_ref=dst, send_sem=ssem, recv_sem=rsem, device_id=device,
            device_id_type=MESH,
        )
        copy.start()
        sends.append(copy)

    def arrived(dst, rsem, ssem):
        pltpu.make_async_remote_copy(
            src_ref=dst, dst_ref=dst, send_sem=ssem, recv_sem=rsem,
            device_id={"row": partner}, device_id_type=MESH,
        ).wait_recv()

    def gather_start(it):
        s_half = surface[...].astype(BF16)
        gat_a[it][core, y, z] = s_half[0:half]
        gat_b[it][core, z, y] = s_half[half:angles]
        if it == 0:
            pl.semaphore_wait(barrier, (nz - 1) + (ny - 1) + 1 + (ncol - 1))
        own_a = gat_a[it].at[core, y, z]
        own_b = gat_b[it].at[core, z, y]
        for o in [k for d in range(nz // 2, 0, -1) for k in sorted({d, nz - d})]:
            send(own_a, own_a, a1_send.at[it, o], a1_recv.at[it, z], {"vol": z_peer(o)})
        for o in range(1, ny):
            dev = {"row": y_peer(o) * CORES + core}
            send(own_b, own_b, b1_send.at[it, o], b1_recv.at[it, y], dev)

    def gather_finish(it):
        for o in range(1, ny):
            src = y_peer(o)
            arrived(gat_b[it].at[core, z, src], b1_recv.at[it, src], b1_send.at[it, o])
        mine_b = gat_b[it].at[core, z]
        for o in [k for d in range(nz // 2, 0, -1) for k in sorted({d, nz - d})]:
            send(mine_b, mine_b, b2_send.at[it, o], b2_recv.at[it, z], {"vol": z_peer(o)})
        send(mine_b, mine_b, cb_send.at[it, 0], cb_recv.at[it, z], {"row": partner})
        for o in range(1, nz):
            src = z_peer(o)
            arrived(gat_a[it].at[core, y, src], a1_recv.at[it, src], a1_send.at[it, o])
        mine_a = gat_a[it].at[core, y]
        for o in range(1, ny):
            dev = {"row": y_peer(o) * CORES + core}
            send(mine_a, mine_a, a2_send.at[it, o], a2_recv.at[it, y], dev)
        send(mine_a, mine_a, ca_send.at[it, 0], ca_recv.at[it, y], {"row": partner})
        for o in [k for d in range(1, nz // 2 + 1) for k in sorted({d, nz - d})]:
            src = z_peer(o)
            ref = gat_b[it].at[core, src]
            arrived(ref, b2_recv.at[it, src], b2_send.at[it, o])
            send(ref, ref, cb_send.at[it, o], cb_recv.at[it, src], {"row": partner})
        for o in range(1, ny):
            src = y_peer(o)
            ref = gat_a[it].at[core, src]
            arrived(ref, a2_recv.at[it, src], a2_send.at[it, o])
            send(ref, ref, ca_send.at[it, o], ca_recv.at[it, src], {"row": partner})
        for o in range(nz):
            src = z_peer(o)
            arrived(gat_b[it].at[1 - core, src], cb_recv.at[it, src], cb_send.at[it, o])
        for o in range(ny):
            src = y_peer(o)
            arrived(gat_a[it].at[1 - core, src], ca_recv.at[it, src], ca_send.at[it, o])

    def piece(it, k, j, v):
        return jnp.concatenate([gat_a[it][k, j, v], gat_b[it][k, v, j]], axis=0)

    def volume_block(b):
        total = dot_nt(field[vol_cols[b, 0]], blocks[b, 0])
        for n in range(1, nnz):
            total += dot_nt(field[vol_cols[b, n]], blocks[b, n])
        return total

    def alive(j):
        return jnp.where(j < bnd_count[0], 1.0, 0.0).astype(F32)

    def traces(it):
        parts = []
        for j in range(slots):
            x_half = volume_block(j).astype(BF16)
            parts.append(dot_nn(x_half, couple[j]) * alive(j))
        for m in range(nz):
            total = None
            for j in range(slots):
                term = parts[j] * jnp.where(trace_map[j] == m, 1.0, 0.0).astype(F32)
                total = term if total is None else total + term
            tr_send[it, m] = total.astype(BF16)

    def traces_send(it):
        for o in [k for d in range(nz // 2, 0, -1) for k in sorted({d, nz - d})]:
            dst = z_peer(o)
            send(
                tr_send.at[it, dst], tr_recv.at[it, z], tr_ssem.at[it, o], tr_rsem.at[it, z],
                {"vol": dst},
            )

    def coeffs_of(it):
        def step(index, total):
            v, j = index // ny, index % ny
            for k in range(CORES):
                start = pl.multiple_of((v * ny * CORES + j * CORES + k) * BS, BS)
                total += dot_nt(piece(it, k, j, v), v_mat[:, pl.ds(start, BS)])
            return total

        zero = jnp.zeros((angles, v_mat.shape[0]), F32)
        return lax.fori_loop(0, nz * ny, step, zero, unroll=8)

    def integral_block(it, coeffs, b):
        start = pl.multiple_of(b * BS, BS)
        total = dot_nn(coeffs, u_mat[:, pl.ds(start, BS)])
        for n in range(nears):
            index = near_cols[b, n]
            v, rest = index // (ny * CORES), index % (ny * CORES)
            total += dot_nt(piece(it, rest % CORES, rest // CORES, v), near[b, n])
        return total

    def integral_send(it, coeffs):
        for o in [ncol - 1 - k for k in range(ncol - 1)]:
            dst = col_peer(o)
            row_send[it, dst] = integral_block(it, coeffs, dst).astype(BF16)
            send(
                row_send.at[it, dst], row_recv.at[it, col], row_ssem.at[it, o],
                row_rsem.at[it, col], {"col": dst},
            )
        row_own[...] = integral_block(it, coeffs, col)

    def residual(it):
        for j in range(slots):
            index = trace_map[j]
            current = dot_nt(piece(it, core, y, index), couple[j]) * alive(j)
            field[j] = (rhs4[j].astype(F32) - current).astype(BF16)

    def surface_step(it):
        total = row_own[...] + tr_send[it, z].astype(F32)
        for o in range(1, nz):
            src = z_peer(o)
            arrived(tr_recv.at[it, src], tr_rsem.at[it, src], tr_ssem.at[it, o])
            total += tr_recv[it, src].astype(F32)
        for o in range(1, ncol):
            src = col_peer(o)
            arrived(row_recv.at[it, src], row_rsem.at[it, src], row_ssem.at[it, o])
            total += row_recv[it, src].astype(F32)
        resid = (rhs_surf[...].astype(F32) - total).astype(BF16)
        surface[...] += dot_nt(resid, inverse[...])

    stores = []
    for it in range(ITERS):
        gather_start(it)
        if it == 0:
            for copy in ld_field + ld_rhs4:
                copy.wait()
            ld_blocks.wait()
            ld_couple.wait()
            traces(0)
        gather_finish(it)
        if it == 0:
            ld_v.wait()
            ld_u.wait()
            ld_near.wait()
        coeffs = coeffs_of(it).astype(BF16)
        integral_send(it, coeffs)
        traces_send(it)
        residual(it)
        if it + 1 < ITERS:
            traces(it + 1)
        else:
            ld_rest.wait()
            for b in range(nblk):
                vol_res[b] = volume_block(b)
                copy = pltpu.make_async_copy(
                    vol_res.at[b], vol_out.at[:, b * BS : (b + 1) * BS], store_sem.at[b]
                )
                copy.start()
                stores.append(copy)
        surface_step(it)
    copy = pltpu.make_async_copy(surface, surf_out, store_sem.at[nblk])
    copy.start()
    stores.append(copy)
    for copy in sends:
        copy.wait_send()
    for copy in stores:
        copy.wait()


def local(
    sizes,
    vol_rhs,
    surf_rhs,
    vol_blocks,
    vol_cols,
    coupling,
    trace_map,
    bnd_count,
    surf_inverse,
    near_blocks,
    near_cols,
    far_u,
    far_v,
):
    nz, ny, nx = sizes
    ncol = nx * Y_HALVES
    angles = vol_rhs.shape[0]
    half = angles // 2
    nblk, nnz = vol_cols.shape
    slots = coupling.shape[0]
    rank = far_u.shape[1]
    nears = near_blocks.shape[2]
    smem = pl.BlockSpec(memory_space=pltpu.SMEM)
    hbm = pl.BlockSpec(memory_space=pl.ANY)
    dma = pltpu.SemaphoreType.DMA
    return pl.pallas_call(
        functools.partial(kernel, sizes),
        out_shape=(
            jax.ShapeDtypeStruct((angles, nblk * BS), F32),
            jax.ShapeDtypeStruct((angles, BS), F32),
        ),
        in_specs=[smem] * 4 + [hbm] * 8,
        out_specs=(hbm, hbm),
        scratch_shapes=[
            pltpu.VMEM((slots, angles, BS), BF16),
            pltpu.VMEM((nblk, angles, BS), BF16),
            pltpu.VMEM((angles, BS), BF16),
            pltpu.VMEM((nblk, nnz, BS, BS), BF16),
            pltpu.VMEM((slots, BS, BS), BF16),
            pltpu.VMEM((BS, BS), BF16),
            pltpu.VMEM((ncol, nears, BS, BS), BF16),
            pltpu.VMEM((rank, ncol * BS), BF16),
            pltpu.VMEM((rank, nz * ny * CORES * BS), BF16),
            pltpu.VMEM((CORES, ny, nz, half, BS), BF16),
            pltpu.VMEM((CORES, nz, ny, half, BS), BF16),
            pltpu.VMEM((CORES, ny, nz, half, BS), BF16),
            pltpu.VMEM((CORES, nz, ny, half, BS), BF16),
            pltpu.VMEM((ITERS, nz, angles, BS), BF16),
            pltpu.VMEM((ITERS, nz, angles, BS), BF16),
            pltpu.VMEM((ITERS, ncol, angles, BS), BF16),
            pltpu.VMEM((ITERS, ncol, angles, BS), BF16),
            pltpu.VMEM((angles, BS), F32),
            pltpu.VMEM((angles, BS), F32),
            pltpu.VMEM((nblk, angles, BS), F32),
            dma((nblk + slots + 8,)),
            dma((nblk + 1,)),
            dma((ITERS, nz)),
            dma((ITERS, nz)),
            dma((ITERS, ny)),
            dma((ITERS, ny)),
            dma((ITERS, ny)),
            dma((ITERS, ny)),
            dma((ITERS, nz)),
            dma((ITERS, nz)),
            dma((ITERS, ny)),
            dma((ITERS, ny)),
            dma((ITERS, nz)),
            dma((ITERS, nz)),
            dma((ITERS, nz)),
            dma((ITERS, nz)),
            dma((ITERS, ncol)),
            dma((ITERS, ncol)),
        ],
        compiler_params=pltpu.CompilerParams(
            collective_id=0, has_side_effects=True, vmem_limit_bytes=60 * 2**20
        ),
    )(
        vol_cols,
        trace_map,
        bnd_count,
        near_cols[:, 0],
        vol_rhs,
        surf_rhs,
        vol_blocks,
        coupling,
        surf_inverse,
        near_blocks,
        far_u,
        far_v,
    )


def solution(mesh):
    sizes = (mesh.shape["vol"], mesh.shape["row"] // CORES, mesh.shape["col"] // Y_HALVES)
    everywhere = ("vol", "row", "col")
    in_specs = (
        P(None, everywhere),
        P(None, everywhere),
        P(everywhere, None, None, None),
        P(everywhere, None),
        P(everywhere, None, None),
        P(everywhere),
        P(everywhere),
        P(everywhere, None, None),
        P(("vol", "row"), "col", None, None, None),
        P(("vol", "row"), "col", None),
        P("col", None, ("vol", "row")),
        P(("vol", "row"), "col", None, None),
    )
    out_specs = (P(None, everywhere), P(None, everywhere))
    return jax.shard_map(
        functools.partial(local, sizes), mesh=mesh, in_specs=in_specs, out_specs=out_specs,
        check_vma=False,
    )
```

time: 165 us -> 69.8 us (0.42)
  the two profiles are of different devices: /device:TPU:8 before, /device:TPU:1 now
where the time goes in v1:
time: 69.8 us; the launch traced here: 69.4 us
  Pallas kernels  62.3 us (89%)
  local copies, waits for them, and re-layouts  5.86 us (8%)
  between operations  1.29 us (2%)
    pallas_call x1, Pallas kernels, local(): pl.pallas_call(functools.partial(kernel, sizes), out_shape=(jax.ShapeDtyp...  62.3 us
    unnamed x3, local copies, waits for them, and re-layouts  4.51 us

profile of v1, /device:TPU:1, one launch (start us, length us, event | category | flops | bytes accessed | tf_op | source)
XLA Modules:
  0.0 69.4 jit_solution(1703609638910227630)
XLA Ops:
  1.3 1.3 %copy.15.near_cols = s32[8,4]{1,0:T(8,128)} copy(s32[8,4]{0,1:T(4,128)} %bitcast.1) | data formatting | bytes 256 | tf_op jit(solution)/shard_map/squeeze | solution.py:408
  2.6 1.4 %copy.14.vol_cols = s32[12,7]{1,0:T(8,128)} copy(s32[12,7]{0,1:T(8,128)} %param.15) | data formatting | bytes 672 | tf_op args[3]
  4.0 62.3 %shard_map.131 = (f32[64,1536]{1,0:T(8,128)}, f32[64,128]{1,0:T(8,128)}) custom-call(s32[12,7]{1,0:T(8,128)} %copy.14.vol_cols, s32[4]{0:T(128)} %trace_map.1, s32[1]{0:T(128)S(6)} %copy.18.bnd_count, s32[8,4]{1,0:T(8,128)} %copy.15.near_cols, bf16[64,1536]{1,0:T(8,128)(2,1)} %vol_rhs.1, bf16[64,128]{1,0:T(8,128)(2,1)} %surf_rhs.1, ...), custom_call_target="tpu_custom_call" | custom-call | tf_op jit(solution)/shard_map/pallas_call | solution.py:353
  66.3 1.8 %copy.19 = f32[64,1536]{1,0:T(8,128)} copy(f32[64,1536]{1,0:T(8,128)} %get-tuple-element.4) | data formatting | bytes 786432
  68.1 1.4 %copy.20 = f32[64,128]{1,0:T(8,128)} copy(f32[64,128]{1,0:T(8,128)} %get-tuple-element.5) | data formatting | bytes 65536

commit v2 on v1

v2 whole, which is shorter than its diff:
```python
import functools

import jax
import jax.numpy as jnp
from jax import lax
from jax.experimental import pallas as pl
from jax.experimental.pallas import tpu as pltpu
from jax.sharding import PartitionSpec as P

BS = 128
ITERS = 2
CORES = 2
Y_HALVES = 2
MESH = pl.DeviceIdType.MESH
F32 = jnp.float32
BF16 = jnp.bfloat16


def dot_nt(a, b):
    return lax.dot_general(a, b, (((1,), (1,)), ((), ())), preferred_element_type=F32)


def dot_nn(a, b):
    return lax.dot_general(a, b, (((1,), (0,)), ((), ())), preferred_element_type=F32)


def kernel(
    sizes,
    vol_cols_hbm,
    trace_map_hbm,
    bnd_count_hbm,
    near_cols_hbm,
    vol_rhs,
    surf_rhs,
    vol_blocks,
    coupling,
    surf_inverse,
    near_blocks,
    far_u,
    far_v,
    vol_out,
    surf_out,
    vol_cols,
    trace_map,
    bnd_count,
    near_cols,
    rhs4,
    field,
    rhs_surf,
    blocks,
    couple,
    inverse,
    near,
    u_mat,
    v_mat,
    gat0,
    gat1,
    tr_send,
    tr_recv,
    row_send,
    row_recv,
    row_own,
    surface,
    load_sem,
    zo_send,
    zo_recv,
    yo_send,
    yo_recv,
    af_send,
    af_recv,
    bf_send,
    bf_recv,
    co_send,
    co_recv,
    tr_ssem,
    tr_rsem,
    row_ssem,
    row_rsem,
):
    gat = (gat0, gat1)
    nz, ny, nx = sizes
    ncol = nx * Y_HALVES
    angles = rhs_surf.shape[0]
    half = angles // 2
    nblk = field.shape[0]
    nnz = blocks.shape[1]
    slots = couple.shape[0]
    nears = near.shape[1]

    z = lax.axis_index("vol")
    row = lax.axis_index("row")
    col = lax.axis_index("col")
    y, core = row // CORES, row % CORES
    x, y_hi = col // Y_HALVES, col % Y_HALVES

    def z_peer(o):
        return lax.rem(z + o, nz)

    def y_peer(o):
        return lax.rem(y + o, ny)

    def col_peer(o):
        return lax.rem(x + o // Y_HALVES, nx) * Y_HALVES + lax.rem(y_hi + o % Y_HALVES, Y_HALVES)

    partner = y * CORES + (1 - core)

    loads = []

    def load(src, dst):
        copy = pltpu.make_async_copy(src, dst, load_sem.at[len(loads)])
        copy.start()
        loads.append(copy)
        return copy

    ld_rhs_surf = load(surf_rhs, rhs_surf)
    ld_inverse = load(surf_inverse.at[0], inverse)

    barrier = pltpu.get_barrier_semaphore()
    for o in range(1, nz):
        pl.semaphore_signal(barrier, inc=1, device_id={"vol": z_peer(o)}, device_id_type=MESH)
    for o in range(1, ny):
        pl.semaphore_signal(
            barrier, inc=1, device_id={"row": y_peer(o) * CORES + core}, device_id_type=MESH
        )
    pl.semaphore_signal(barrier, inc=1, device_id={"row": partner}, device_id_type=MESH)
    for o in range(1, ncol):
        pl.semaphore_signal(barrier, inc=1, device_id={"col": col_peer(o)}, device_id_type=MESH)

    ld_tables = [
        load(vol_cols_hbm, vol_cols),
        load(trace_map_hbm, trace_map),
        load(bnd_count_hbm, bnd_count),
        load(near_cols_hbm, near_cols),
    ]
    ld_field = [load(vol_rhs.at[:, b * BS : (b + 1) * BS], field.at[b]) for b in range(nblk)]
    ld_rhs4 = [load(vol_rhs.at[:, b * BS : (b + 1) * BS], rhs4.at[b]) for b in range(slots)]
    ld_blocks = load(vol_blocks.at[0:slots], blocks.at[0:slots])
    ld_couple = load(coupling, couple)
    ld_v = load(far_v.at[0, 0], v_mat)
    ld_u = load(far_u.at[0], u_mat)
    ld_near = load(near_blocks.at[:, 0], near)
    ld_rest = load(vol_blocks.at[slots:nblk], blocks.at[slots:nblk])

    ld_rhs_surf.wait()
    ld_inverse.wait()
    surface[...] = dot_nt(rhs_surf[...], inverse[...])

    sends = []

    def send(src, dst, ssem, rsem, device):
        copy = pltpu.make_async_remote_copy(
            src_ref=src, dst_ref=dst, send_sem=ssem, recv_sem=rsem, device_id=device,
            device_id_type=MESH,
        )
        copy.start()
        sends.append(copy)

    def arrived(dst, rsem, ssem):
        pltpu.make_async_remote_copy(
            src_ref=dst, dst_ref=dst, send_sem=ssem, recv_sem=rsem,
            device_id={"row": partner}, device_id_type=MESH,
        ).wait_recv()

    z_far_first = [k for d in range(nz // 2, 0, -1) for k in sorted({d, nz - d})]
    z_near_first = z_far_first[::-1]
    y_order = sorted(range(1, ny), key=lambda o: abs(o - ny / 2))

    def gather_start(it):
        own = gat[it].at[core, z, y]
        own[...] = surface[...].astype(BF16)
        if it == 0:
            pl.semaphore_wait(barrier, (nz - 1) + (ny - 1) + 1 + (ncol - 1))
        for o in z_far_first:
            send(own, own, zo_send.at[it, o], zo_recv.at[it, z], {"vol": z_peer(o)})
        for o in y_order:
            dev = {"row": y_peer(o) * CORES + core}
            send(own, own, yo_send.at[it, o], yo_recv.at[it, y], dev)
        send(own, own, co_send.at[it, 0, 0], co_recv.at[it, z, y], {"row": partner})

    def from_z(it, oz):
        src = z_peer(oz)
        ref = gat[it].at[core, src, y]
        arrived(ref, zo_recv.at[it, src], zo_send.at[it, oz])
        first = ref.at[0:half]
        for oy in y_order:
            dev = {"row": y_peer(oy) * CORES + core}
            send(first, first, af_send.at[it, oz, oy], af_recv.at[it, src, y], dev)
        send(ref, ref, co_send.at[it, oz, 0], co_recv.at[it, src, y], {"row": partner})

    def from_y(it, oy):
        src = y_peer(oy)
        ref = gat[it].at[core, z, src]
        arrived(ref, yo_recv.at[it, src], yo_send.at[it, oy])
        second = ref.at[half:angles]
        for oz in z_far_first:
            send(
                second, second, bf_send.at[it, oz, oy], bf_recv.at[it, z, src],
                {"vol": z_peer(oz)},
            )
        send(ref, ref, co_send.at[it, 0, oy], co_recv.at[it, z, src], {"row": partner})

    def from_both(it, oz, oy):
        z_src, y_src = z_peer(oz), y_peer(oy)
        ref = gat[it].at[core, z_src, y_src]
        arrived(ref.at[0:half], af_recv.at[it, z_src, y_src], af_send.at[it, oz, oy])
        arrived(ref.at[half:angles], bf_recv.at[it, z_src, y_src], bf_send.at[it, oz, oy])
        send(ref, ref, co_send.at[it, oz, oy], co_recv.at[it, z_src, y_src], {"row": partner})

    def far_part(it, k, oz):
        v = z_peer(oz)
        lhs, rhs = [], []
        for j in range(ny):
            lhs.append(gat[it][k, v, j])
            start = pl.multiple_of((v * ny * CORES + j * CORES + k) * BS, BS)
            rhs.append(v_mat[:, pl.ds(start, BS)])
        return dot_nt(jnp.concatenate(lhs, axis=1), jnp.concatenate(rhs, axis=1))

    def gather_finish(it):
        legs = [(d, 1, o) for o in z_near_first for d in [2 * min(o, nz - o)]]
        legs += [(3 if o == ny // 2 else 5, 0, o) for o in y_order]
        for _, along_z, o in sorted(legs):
            if along_z:
                from_z(it, o)
            else:
                from_y(it, o)
        for oz in z_near_first:
            for oy in y_order:
                from_both(it, oz, oy)
        if it == 0:
            ld_v.wait()
        total = None
        for oz in [0] + z_near_first:
            term = far_part(it, core, oz)
            total = term if total is None else total + term
        for oz in [0] + z_near_first:
            v = z_peer(oz)
            for oy in [0] + y_order:
                j = y_peer(oy)
                arrived(gat[it].at[1 - core, v, j], co_recv.at[it, v, j], co_send.at[it, oz, oy])
            total += far_part(it, 1 - core, oz)
        return total.astype(BF16)

    def volume_block(b):
        lhs = jnp.concatenate([field[vol_cols[n, b]] for n in range(nnz)], axis=1)
        rhs = jnp.concatenate([blocks[b, n] for n in range(nnz)], axis=1)
        return dot_nt(lhs, rhs)

    def alive(j):
        return jnp.where(j < bnd_count[0], 1.0, 0.0).astype(F32)

    def traces(it):
        parts = []
        for j in range(slots):
            x_half = volume_block(j).astype(BF16)
            parts.append(dot_nn(x_half, couple[j]) * alive(j))
        for m in range(nz):
            total = None
            for j in range(slots):
                term = parts[j] * jnp.where(trace_map[j] == m, 1.0, 0.0).astype(F32)
                total = term if total is None else total + term
            tr_send[it, m] = total.astype(BF16)

    def traces_send(it):
        for o in [k for d in range(nz // 2, 0, -1) for k in sorted({d, nz - d})]:
            dst = z_peer(o)
            send(
                tr_send.at[it, dst], tr_recv.at[it, z], tr_ssem.at[it, o], tr_rsem.at[it, z],
                {"vol": dst},
            )

    def integral_block(it, coeffs, b):
        start = pl.multiple_of(b * BS, BS)
        lhs, rhs = [], []
        for n in range(nears):
            index = near_cols[n, b]
            v, rest = index // (ny * CORES), index % (ny * CORES)
            lhs.append(gat[it][rest % CORES, v, rest // CORES])
            rhs.append(near[b, n])
        total = dot_nt(jnp.concatenate(lhs, axis=1), jnp.concatenate(rhs, axis=1))
        return total + dot_nn(coeffs, u_mat[:, pl.ds(start, BS)])

    col_order = sorted(
        range(1, ncol), key=lambda o: (-(o % Y_HALVES), abs(o // Y_HALVES - nx / 2))
    )

    def integral_send(it, coeffs):
        for o in col_order:
            dst = col_peer(o)
            row_send[it, dst] = integral_block(it, coeffs, dst).astype(BF16)
            send(
                row_send.at[it, dst], row_recv.at[it, col], row_ssem.at[it, o],
                row_rsem.at[it, col], {"col": dst},
            )
        row_own[...] = integral_block(it, coeffs, col)

    def residual(it):
        for j in range(slots):
            index = trace_map[j]
            current = dot_nt(gat[it][core, index, y], couple[j]) * alive(j)
            field[j] = (rhs4[j].astype(F32) - current).astype(BF16)

    def surface_step(it):
        total = row_own[...] + tr_send[it, z].astype(F32)
        for o in range(1, nz):
            src = z_peer(o)
            arrived(tr_recv.at[it, src], tr_rsem.at[it, src], tr_ssem.at[it, o])
            total += tr_recv[it, src].astype(F32)
        for o in range(1, ncol):
            src = col_peer(o)
            arrived(row_recv.at[it, src], row_rsem.at[it, src], row_ssem.at[it, o])
            total += row_recv[it, src].astype(F32)
        resid = (rhs_surf[...].astype(F32) - total).astype(BF16)
        surface[...] += dot_nt(resid, inverse[...])

    for it in range(ITERS):
        if it == 0:
            for copy in ld_tables + ld_field + ld_rhs4:
                copy.wait()
            ld_blocks.wait()
            ld_couple.wait()
            traces(0)
        gather_start(it)
        coeffs = gather_finish(it)
        if it == 0:
            ld_u.wait()
            ld_near.wait()
        integral_send(it, coeffs)
        traces_send(it)
        residual(it)
        if it + 1 < ITERS:
            traces(it + 1)
        else:
            ld_rest.wait()
            for b in range(nblk):
                vol_out[:, b * BS : (b + 1) * BS] = volume_block(b)
        surface_step(it)
    surf_out[...] = surface[...]
    for copy in sends:
        copy.wait_send()


def in_hbm(x):
    if x.size == 1:
        return x
    return pltpu.with_memory_space_constraint(x, pltpu.HBM)


def local(
    sizes,
    vol_rhs,
    surf_rhs,
    vol_blocks,
    vol_cols,
    coupling,
    trace_map,
    bnd_count,
    surf_inverse,
    near_blocks,
    near_cols,
    far_u,
    far_v,
):
    nz, ny, nx = sizes
    ncol = nx * Y_HALVES
    angles = vol_rhs.shape[0]
    nblk, nnz = vol_cols.shape
    slots = coupling.shape[0]
    rank = far_u.shape[1]
    nears = near_blocks.shape[2]
    hbm = pl.BlockSpec(memory_space=pltpu.HBM)
    dma = pltpu.SemaphoreType.DMA
    return pl.pallas_call(
        functools.partial(kernel, sizes),
        out_shape=(
            jax.ShapeDtypeStruct((angles, nblk * BS), F32),
            jax.ShapeDtypeStruct((angles, BS), F32),
        ),
        in_specs=[hbm] * 2 + [pl.BlockSpec(memory_space=pl.ANY)] + [hbm] * 9,
        out_specs=(pl.BlockSpec(memory_space=pltpu.VMEM),) * 2,
        scratch_shapes=[
            pltpu.SMEM((nnz, nblk), jnp.int32),
            pltpu.SMEM((slots,), jnp.int32),
            pltpu.SMEM((1,), jnp.int32),
            pltpu.SMEM((nears, ncol), jnp.int32),
            pltpu.VMEM((slots, angles, BS), BF16),
            pltpu.VMEM((nblk, angles, BS), BF16),
            pltpu.VMEM((angles, BS), BF16),
            pltpu.VMEM((nblk, nnz, BS, BS), BF16),
            pltpu.VMEM((slots, BS, BS), BF16),
            pltpu.VMEM((BS, BS), BF16),
            pltpu.VMEM((ncol, nears, BS, BS), BF16),
            pltpu.VMEM((rank, ncol * BS), BF16),
            pltpu.VMEM((rank, nz * ny * CORES * BS), BF16),
            pltpu.VMEM((CORES, nz, ny, angles, BS), BF16),
            pltpu.VMEM((CORES, nz, ny, angles, BS), BF16),
            pltpu.VMEM((ITERS, nz, angles, BS), BF16),
            pltpu.VMEM((ITERS, nz, angles, BS), BF16),
            pltpu.VMEM((ITERS, ncol, angles, BS), BF16),
            pltpu.VMEM((ITERS, ncol, angles, BS), BF16),
            pltpu.VMEM((angles, BS), F32),
            pltpu.VMEM((angles, BS), F32),
            dma((nblk + slots + 12,)),
            dma((ITERS, nz)),
            dma((ITERS, nz)),
            dma((ITERS, ny)),
            dma((ITERS, ny)),
            dma((ITERS, nz, ny)),
            dma((ITERS, nz, ny)),
            dma((ITERS, nz, ny)),
            dma((ITERS, nz, ny)),
            dma((ITERS, nz, ny)),
            dma((ITERS, nz, ny)),
            dma((ITERS, nz)),
            dma((ITERS, nz)),
            dma((ITERS, ncol)),
            dma((ITERS, ncol)),
        ],
        compiler_params=pltpu.CompilerParams(
            collective_id=0, has_side_effects=True, vmem_limit_bytes=16 * 2**20
        ),
    )(*map(
        in_hbm, (vol_cols.T,
        trace_map,
        bnd_count,
        near_cols[:, 0].T,
        vol_rhs,
        surf_rhs,
        vol_blocks,
        coupling,
        surf_inverse,
        near_blocks,
        far_u,
        far_v,
    )))


def solution(mesh):
    sizes = (mesh.shape["vol"], mesh.shape["row"] // CORES, mesh.shape["col"] // Y_HALVES)
    everywhere = ("vol", "row", "col")
    in_specs = (
        P(None, everywhere),
        P(None, everywhere),
        P(everywhere, None, None, None),
        P(everywhere, None),
        P(everywhere, None, None),
        P(everywhere),
        P(everywhere),
        P(everywhere, None, None),
        P(("vol", "row"), "col", None, None, None),
        P(("vol", "row"), "col", None),
        P("col", None, ("vol", "row")),
        P(("vol", "row"), "col", None, None),
    )
    out_specs = (P(None, everywhere), P(None, everywhere))
    return jax.shard_map(
        functools.partial(local, sizes), mesh=mesh, in_specs=in_specs, out_specs=out_specs,
        check_vma=False,
    )
```

time: 69.8 us -> 65.1 us (0.933)
  local copies, waits for them, and re-layouts: 5.86 us -> 1.36 us
    unnamed x3 -> x2, local copies, waits for them, and re-layouts: 4.51 us -> 1.36 us
    squeeze x1 -> x0, local copies, waits for them, and re-layouts: 1.35 us -> none  [local(): near_cols[:, 0]]
where the time goes in v2:
time: 65.1 us; the launch traced here: 64.9 us
  Pallas kernels  62.2 us (96%)
  local copies, waits for them, and re-layouts  1.36 us (2%)
  between operations  1.29 us (2%)
    pallas_call x1, Pallas kernels, local(): pl.pallas_call(functools.partial(kernel, sizes), out_shape=(jax.ShapeDtyp...  62.2 us
    unnamed x2, local copies, waits for them, and re-layouts  1.36 us

profile of v2, /device:TPU:1, one launch (start us, length us, event | category | flops | bytes accessed | tf_op | source)
XLA Modules:
  0.0 64.9 jit_solution(1479830301127434658)
XLA Ops:
  1.3 62.2 %shard_map.131 = (f32[64,1536]{1,0:T(8,128)S(1)}, f32[64,128]{1,0:T(8,128)S(1)}) custom-call(s32[7,12]{1,0:T(8,128)} %bitcast.4, s32[4]{0:T(128)} %trace_map_hbm.1, s32[1]{0:T(128)S(6)} %copy.16.bnd_count_hbm, s32[4,8]{1,0:T(4,128)} %bitcast.5, bf16[64,1536]{1,0:T(8,128)(2,1)} %vol_rhs.1, bf16[64,128]{1,0:T(8,128)(2,1)} %surf_rhs.1, ...), custom_call_target="tpu_custom_call" | custom-call | tf_op jit(solution)/shard_map/pallas_call | solution.py:372
  63.5 0.7 %copy.17 = f32[64,1536]{1,0:T(8,128)} copy(f32[64,1536]{1,0:T(8,128)S(1)} %get-tuple-element.4) | data formatting | bytes 786432
  64.3 0.6 copy.18

commit v3 on v2

--- a/solution.py
+++ b/solution.py
@@ -12,6 +12,8 @@
 CORES = 2
 Y_HALVES = 2
 MESH = pl.DeviceIdType.MESH
+CORNER = {(1, 1): 'AB', (1, 2): 'AB', (2, 1): 'AB', (2, 2): 'AB', (3, 1): 'AB', (3, 2): 'AB', (4, 1): 'AB', (4, 2): 'AB'}
+NEAR_FIRST = True
 F32 = jnp.float32
 BF16 = jnp.bfloat16
 
@@ -165,45 +167,71 @@
     z_near_first = z_far_first[::-1]
     y_order = sorted(range(1, ny), key=lambda o: abs(o - ny / 2))
 
+    def route(oz, oy):
+        return CORNER[min(oz, nz - oz), min(oy, ny - oy)]
+
+    def share(ref, way, path):
+        if way == "AB":
+            return ref.at[0:half] if path == "A" else ref.at[half:angles]
+        return ref
+
+    def at_row(oy):
+        return y_peer(oy) * CORES + core
+
+    z_own_order = z_near_first if NEAR_FIRST else z_far_first
+
     def gather_start(it):
         own = gat[it].at[core, z, y]
         own[...] = surface[...].astype(BF16)
         if it == 0:
             pl.semaphore_wait(barrier, (nz - 1) + (ny - 1) + 1 + (ncol - 1))
-        for o in z_far_first:
+        for o in y_order:
+            send(own, own, yo_send.at[it, o], yo_recv.at[it, y], {"row": at_row(o)})
+        for o in z_own_order:
             send(own, own, zo_send.at[it, o], zo_recv.at[it, z], {"vol": z_peer(o)})
-        for o in y_order:
-            dev = {"row": y_peer(o) * CORES + core}
-            send(own, own, yo_send.at[it, o], yo_recv.at[it, y], dev)
         send(own, own, co_send.at[it, 0, 0], co_recv.at[it, z, y], {"row": partner})
+        for oz in z_far_first:
+            for oy in y_order:
+                if route(oz, oy) == "D":
+                    send(
+                        own, own, af_send.at[it, oz, oy], af_recv.at[it, z, y],
+                        {"vol": z_peer(oz), "row": at_row(oy)},
+                    )
 
     def from_z(it, oz):
         src = z_peer(oz)
         ref = gat[it].at[core, src, y]
         arrived(ref, zo_recv.at[it, src], zo_send.at[it, oz])
-        first = ref.at[0:half]
         for oy in y_order:
-            dev = {"row": y_peer(oy) * CORES + core}
-            send(first, first, af_send.at[it, oz, oy], af_recv.at[it, src, y], dev)
+            if "A" in route(oz, oy):
+                part = share(ref, route(oz, oy), "A")
+                send(
+                    part, part, af_send.at[it, oz, oy], af_recv.at[it, src, y],
+                    {"row": at_row(oy)},
+                )
         send(ref, ref, co_send.at[it, oz, 0], co_recv.at[it, src, y], {"row": partner})
 
     def from_y(it, oy):
         src = y_peer(oy)
         ref = gat[it].at[core, z, src]
         arrived(ref, yo_recv.at[it, src], yo_send.at[it, oy])
-        second = ref.at[half:angles]
         for oz in z_far_first:
-            send(
-                second, second, bf_send.at[it, oz, oy], bf_recv.at[it, z, src],
-                {"vol": z_peer(oz)},
-            )
+            if "B" in route(oz, oy):
+                part = share(ref, route(oz, oy), "B")
+                send(
+                    part, part, bf_send.at[it, oz, oy], bf_recv.at[it, z, src],
+                    {"vol": z_peer(oz)},
+                )
         send(ref, ref, co_send.at[it, 0, oy], co_recv.at[it, z, src], {"row": partner})
 
     def from_both(it, oz, oy):
         z_src, y_src = z_peer(oz), y_peer(oy)
         ref = gat[it].at[core, z_src, y_src]
-        arrived(ref.at[0:half], af_recv.at[it, z_src, y_src], af_send.at[it, oz, oy])
-        arrived(ref.at[half:angles], bf_recv.at[it, z_src, y_src], bf_send.at[it, oz, oy])
+        way = route(oz, oy)
+        if way != "B":
+            arrived(share(ref, way, "A"), af_recv.at[it, z_src, y_src], af_send.at[it, oz, oy])
+        if "B" in way:
+            arrived(share(ref, way, "B"), bf_recv.at[it, z_src, y_src], bf_send.at[it, oz, oy])
         send(ref, ref, co_send.at[it, oz, oy], co_recv.at[it, z_src, y_src], {"row": partner})
 
     def far_part(it, k, oz):
@@ -217,7 +245,7 @@
 
     def gather_finish(it):
         legs = [(d, 1, o) for o in z_near_first for d in [2 * min(o, nz - o)]]
-        legs += [(3 if o == ny // 2 else 5, 0, o) for o in y_order]
+        legs += [(3, 0, o) for o in y_order]
         for _, along_z, o in sorted(legs):
             if along_z:
                 from_z(it, o)

time: 65.1 us -> 62.6 us (0.962)
  Pallas kernels: 62.2 us -> 59.8 us
    pallas_call x1, Pallas kernels: 62.2 us -> 59.8 us  [local(): pl.pallas_call(functools.partial(kernel, sizes), out_shape=(jax.ShapeDtyp...]
where the time goes in v3:
time: 62.6 us; the launch traced here: 62.4 us
  Pallas kernels  59.8 us (96%)
  local copies, waits for them, and re-layouts  1.36 us (2%)
  between operations  1.29 us (2%)
    pallas_call x1, Pallas kernels, local(): pl.pallas_call(functools.partial(kernel, sizes), out_shape=(jax.ShapeDtyp...  59.8 us
    unnamed x2, local copies, waits for them, and re-layouts  1.36 us

profile of v3, /device:TPU:1, one launch (start us, length us, event | category | flops | bytes accessed | tf_op | source)
XLA Modules:
  0.0 62.4 jit_solution(9881653632452020339)
XLA Ops:
  1.3 59.8 %shard_map.131 = (f32[64,1536]{1,0:T(8,128)S(1)}, f32[64,128]{1,0:T(8,128)S(1)}) custom-call(s32[7,12]{1,0:T(8,128)} %bitcast.4, s32[4]{0:T(128)} %trace_map_hbm.1, s32[1]{0:T(128)S(6)} %copy.16.bnd_count_hbm, s32[4,8]{1,0:T(4,128)} %bitcast.5, bf16[64,1536]{1,0:T(8,128)(2,1)} %vol_rhs.1, bf16[64,128]{1,0:T(8,128)(2,1)} %surf_rhs.1, ...), custom_call_target="tpu_custom_call" | custom-call | tf_op jit(solution)/shard_map/pallas_call | solution.py:400
  61.1 0.7 %copy.17 = f32[64,1536]{1,0:T(8,128)} copy(f32[64,1536]{1,0:T(8,128)S(1)} %get-tuple-element.4) | data formatting | bytes 786432
  61.8 0.6 copy.18

commit v4 on v3

--- a/solution.py
+++ b/solution.py
@@ -349,6 +349,7 @@
             traces(0)
         gather_start(it)
         coeffs = gather_finish(it)
+        early = len(sends)
         if it == 0:
             ld_u.wait()
             ld_near.wait()
@@ -361,9 +362,12 @@
             ld_rest.wait()
             for b in range(nblk):
                 vol_out[:, b * BS : (b + 1) * BS] = volume_block(b)
+        if it + 1 == ITERS:
+            for copy in sends[:early]:
+                copy.wait_send()
         surface_step(it)
     surf_out[...] = surface[...]
-    for copy in sends:
+    for copy in sends[early:]:
         copy.wait_send()
 
 

time: 62.6 us -> 62.3 us (level)
  no operation moved by 1% of the time
where the time goes in v4:
time: 62.3 us; the launch traced here: 62.1 us
  Pallas kernels  59.5 us (96%)
  local copies, waits for them, and re-layouts  1.36 us (2%)
  between operations  1.29 us (2%)
    pallas_call x1, Pallas kernels, local(): pl.pallas_call(functools.partial(kernel, sizes), out_shape=(jax.ShapeDtyp...  59.5 us
    unnamed x2, local copies, waits for them, and re-layouts  1.36 us

profile of v4, /device:TPU:1, one launch (start us, length us, event | category | flops | bytes accessed | tf_op | source)
XLA Modules:
  0.0 62.1 jit_solution(12625796784744874480)
XLA Ops:
  1.3 59.5 %shard_map.131 = (f32[64,1536]{1,0:T(8,128)S(1)}, f32[64,128]{1,0:T(8,128)S(1)}) custom-call(s32[7,12]{1,0:T(8,128)} %bitcast.4, s32[4]{0:T(128)} %trace_map_hbm.1, s32[1]{0:T(128)S(6)} %copy.16.bnd_count_hbm, s32[4,8]{1,0:T(4,128)} %bitcast.5, bf16[64,1536]{1,0:T(8,128)(2,1)} %vol_rhs.1, bf16[64,128]{1,0:T(8,128)(2,1)} %surf_rhs.1, ...), custom_call_target="tpu_custom_call" | custom-call | tf_op jit(solution)/shard_map/pallas_call | solution.py:404
  60.8 0.7 %copy.17 = f32[64,1536]{1,0:T(8,128)} copy(f32[64,1536]{1,0:T(8,128)S(1)} %get-tuple-element.4) | data formatting | bytes 786432
  61.5 0.6 copy.18
